TPU v7x, 32 devices: a whole 2x2x4 slice. The times are simulated.
32 devices in a mesh: groups: 2 (over y), zone: 4 (over x, core), tile: 4 (over z).
Axes of the slice: x: 2, y: 2, z: 4, core: 2. Of those that a mesh axis runs over, the one named last changes fastest.
Arguments:
- backscatter: bfloat16 [8, 2, 256, 512], P(('groups', 'zone'), None, 'tile'), parts along dimension 0, may hold values from -6 to 6
- row_bank: bfloat16 [16, 128, 128], replicated, may hold values from -0.3125 to 0.3125
- row_index: int32 [8, 4, 3], P(('groups', 'zone')), parts along dimension 0, may hold values from 0 to 3
- row_pick: int32 [8, 4, 3], P(('groups', 'zone')), parts along dimension 0, may hold values from 0 to 15
- row_mask: int32 [8, 4, 3], P(('groups', 'zone')), parts along dimension 0, may hold values 0 or 1
- column_bank: bfloat16 [16, 128, 128], replicated, may hold values from -0.3125 to 0.3125
- column_index: int32 [8, 2, 3], P(('groups', 'zone')), parts along dimension 0, may hold values from 0 to 1
- column_pick: int32 [8, 2, 3], P(('groups', 'zone')), parts along dimension 0, may hold values from 0 to 15
- column_mask: int32 [8, 2, 3], P(('groups', 'zone')), parts along dimension 0, may hold values 0 or 1
Outputs:
- geocoded: bfloat16 [8, 2, 256, 512], P(('groups', 'zone'), None, None, 'tile'), parts along dimension 0
There are 2 independent parts, one for each index of `groups`. A program takes and returns all parts, laid end to end along the dimension named above; an argument that names none is the same for every part. Nothing has to cross between parts.
All inputs are finite; a program needn't handle non-finite values. No bound on the sum of `row_mask` or of `column_mask` on one device may be relied on, other than what follows from the above.
Results may differ from a plain program's by a relative error of at most 0.0049.
Values may be sent and summed in bfloat16 or wider, within the bound.
No kernel may reach another device: no remote copies, remote signals or barrier semaphores. Data moves between devices by JAX's collectives and lax.ppermute only.
A program may use at most 64 MiB of HBM per device.

v0:
```python
import jax
import jax.numpy as jnp
from jax import lax
from jax.sharding import PartitionSpec as P

BLOCK = 128
EDGE = 64


def passed_along(block, axis, distance):
    devices = range(lax.axis_size(axis))
    route = [(i - distance, i) for i in devices if i - distance in devices]
    return lax.ppermute(block, axis, route)


def swap_panels(top_panel, bottom_panel):
    from_below = passed_along(top_panel, "zone", -1)
    from_above = passed_along(bottom_panel, "zone", 1)
    zone_index = lax.axis_index("zone")
    last_zone = lax.axis_size("zone") - 1
    feather = ((jnp.arange(EDGE, dtype=jnp.float32) + 0.5) / EDGE)[:, None]
    lower_blend = (
        (1.0 - feather) * bottom_panel.astype(jnp.float32)
        + feather * from_below.astype(jnp.float32)
    ).astype(jnp.bfloat16)
    upper_blend = (
        (1.0 - feather) * from_above.astype(jnp.float32) + feather * top_panel.astype(jnp.float32)
    ).astype(jnp.bfloat16)
    new_bottom = jnp.where(zone_index < last_zone, lower_blend, bottom_panel)
    new_top = jnp.where(zone_index > 0, upper_blend, top_panel)
    return (new_top, new_bottom)


def on_device(
    backscatter,
    row_bank,
    row_index,
    row_pick,
    row_mask,
    column_bank,
    column_index,
    column_pick,
    column_mask,
):
    image = backscatter[0]
    channels, lin_dev, samples = image.shape
    column_blocks = samples // BLOCK
    blocks = image.reshape(channels, lin_dev, column_blocks, BLOCK)
    gathered = blocks[:, :, row_index[0], :]
    row_weights = row_bank[row_pick[0]] * row_mask[0].astype(jnp.bfloat16)[:, :, None, None]
    along_samples = jnp.einsum(
        "clqbi,qbij->clqj", gathered, row_weights, preferred_element_type=jnp.float32
    )
    along_samples = along_samples.astype(jnp.bfloat16).reshape(channels, lin_dev, samples)
    line_blocks = column_index.shape[1]
    rows = line_blocks * BLOCK
    column_weights = (
        column_bank[column_pick[0]] * column_mask[0].astype(jnp.bfloat16)[:, :, None, None]
    )
    band_table = column_index[0]
    every_id = jnp.arange(line_blocks, dtype=jnp.int32)
    moved = lax.all_to_all(along_samples, "tile", split_axis=2, concat_axis=1, tiled=True)
    count = moved.shape[0]
    line_tiles = moved.reshape(count, line_blocks, BLOCK, BLOCK)
    picked = line_tiles[:, band_table[every_id]]
    result = jnp.einsum(
        "crbik,rboi->crok", picked, column_weights[every_id], preferred_element_type=jnp.float32
    )
    result = result.astype(jnp.bfloat16).reshape(count, every_id.shape[0] * BLOCK, BLOCK)
    new_top, new_bottom = swap_panels(result[:, :EDGE], result[:, rows - EDGE :])
    gridded = jnp.concatenate([new_top, result[:, EDGE : rows - EDGE], new_bottom], axis=1)
    return gridded[None]


def solution(mesh):
    in_specs = (
        P(("groups", "zone"), None, "tile", None),
        P(),
        P(("groups", "zone"), None, None),
        P(("groups", "zone"), None, None),
        P(("groups", "zone"), None, None),
        P(),
        P(("groups", "zone"), None, None),
        P(("groups", "zone"), None, None),
        P(("groups", "zone"), None, None),
    )
    out_specs = P(("groups", "zone"), None, None, "tile")
    return jax.shard_map(
        on_device, mesh=mesh, in_specs=in_specs, out_specs=out_specs, check_vma=False
    )
```

profile of v0, /device:TPU:1, one launch (start us, length us, event | category | flops | bytes accessed | tf_op | source)
XLA Modules:
  0.0 29.0 jit_solution(11059921443978826120)
XLA Ops:
  0.0 1.0 %reshape_squeeze.3 = bf16[2,64,4,128]{3,2,1,0:T(4,128)(2,1)S(1)} reshape(bf16[1,2,64,512]{3,2,1,0:T(8,128)(2,1)} %param.9) | data formatting | bytes 262144 | tf_op jit(solution)/shard_map/reshape;squeeze | solution.py:48
  1.0 0.6 %copy-done.2 = s32[1,4,3]{1,0,2:T(1,128)S(1)} copy-done((s32[1,4,3]{1,0,2:T(1,128)S(1)}, s32[1,4,3]{1,0,2:T(1,128)}, u32[]{:S(2)}) %copy-start.2) | copy-done | bytes 72
  1.9 0.7 %copy-done.3 = s32[1,4,3]{1,0,2:T(1,128)S(1)} copy-done((s32[1,4,3]{1,0,2:T(1,128)S(1)}, s32[1,4,3]{1,0,2:T(1,128)}, u32[]{:S(2)}) %copy-start.3) | copy-done | bytes 72
  2.8 0.7 %copy-done.4 = s32[1,4,3]{1,0,2:T(1,128)S(1)} copy-done((s32[1,4,3]{1,0,2:T(1,128)S(1)}, s32[1,4,3]{1,0,2:T(1,128)}, u32[]{:S(2)}) %copy-start.4) | copy-done | bytes 72
  3.5 0.6 %gather_fusion.3 = bf16[12,2,64,128]{3,2,1,0:T(8,128)(2,1)S(1)} fusion(bf16[2,64,4,128]{3,1,2,0:T(8,128)(2,1)S(1)} %copy.42, s32[1024]{0:T(1024)S(1)} %pad_clamp_fusion.1), kind=kCustom, calls=%fused_computation.3 | custom fusion | bytes 786480 | tf_op jit(solution)/shard_map/gather | solution.py:49
  4.2 0.6 %gather_fusion.2 = bf16[12,128,128]{2,1,0:T(8,128)(2,1)S(1)} fusion(bf16[16,128,128]{2,1,0:T(8,128)(2,1)S(1)} %copy-done, s32[1024]{0:T(1024)S(1)} %pad_clamp_fusion.2), kind=kCustom, calls=%fused_computation.2 | custom fusion | bytes 786480 | tf_op jit(solution)/shard_map/gather | solution.py:50
  4.8 0.3 %fusion.2 = bf16[2,64,4,128]{3,1,0,2:T(8,128)(2,1)S(1)} fusion(bf16[2,64,4,3,128]{4,1,0,3,2:T(8,128)(2,1)S(1)} %bitcast.85, bf16[4,3,128,128]{3,2,1,0:T(8,128)(2,1)S(1)} %bitcast.87, bf16[4,3]{1,0:T(4,128)(2,1)S(1)} %bitcast.89), kind=kOutput, calls=%fused_computation.10 | convolution fusion | flops 51183616 | bytes 917528 | tf_op jit(solution)/shard_map/clqbi,qbij->clqj/dot_general | solution.py:51
  5.2 0.2 copy.54
  5.3 0.9 %reshape.188 = bf16[4,2,8192]{2,1,0:T(2,128)(2,1)} reshape(bf16[512,2,64]{2,1,0:T(2,128)(2,1)S(1)} %bitcast.79) | data formatting | bytes 262144
  6.2 5.4 %all-to-all-start = ((bf16[4,2,8192]{2,1,0:T(2,128)(2,1)}), bf16[4,2,8192]{2,1,0:T(2,128)(2,1)S(1)}, u32[]{:S(2)}, u32[]{:S(2)}) async-start(bf16[4,2,8192]{2,1,0:T(2,128)(2,1)} %reshape.188), calls=%async_computation | async-start | bytes 262144 | tf_op jit(solution)/shard_map/all_to_all | solution.py:62
  11.7 0.7 %copy-done.5 = s32[1,2,3]{2,1,0:T(2,128)S(1)} copy-done((s32[1,2,3]{2,1,0:T(2,128)S(1)}, s32[1,2,3]{2,1,0:T(2,128)}, u32[]{:S(2)}) %copy-start.5) | copy-done | bytes 48
  12.4 0.7 %copy-done.6 = s32[1,2,3]{2,1,0:T(2,128)S(1)} copy-done((s32[1,2,3]{2,1,0:T(2,128)S(1)}, s32[1,2,3]{2,1,0:T(2,128)}, u32[]{:S(2)}) %copy-start.6) | copy-done | bytes 48
  13.1 0.7 %copy-done.1 = s32[1,2,3]{2,1,0:T(2,128)S(1)} copy-done((s32[1,2,3]{2,1,0:T(2,128)S(1)}, s32[1,2,3]{2,1,0:T(2,128)}, u32[]{:S(2)}) %copy-start.1) | copy-done | bytes 48
  13.8 0.6 %gather_fusion.4 = s32[2,3]{1,0:T(2,128)S(1)} fusion(s32[2,3]{1,0:T(2,128)S(1)} %bitcast.88, s32[1024]{0:T(1024)S(1)} %pad_clamp_fusion.3), kind=kCustom, calls=%fused_computation.4 | custom fusion | bytes 56 | tf_op jit(solution)/shard_map/gather | solution.py:65
  14.3 1.6 %gather_fusion = bf16[6,128,128]{2,1,0:T(8,128)(2,1)S(1)} fusion(bf16[16,128,128]{2,1,0:T(8,128)(2,1)} %param.14, s32[1024]{0:T(1024)S(1)} %pad_clamp_fusion.4), kind=kCustom, calls=%fused_computation | custom fusion | bytes 393240 | tf_op jit(solution)/shard_map/gather | solution.py:58
  16.1 0.6 %gather_fusion.1 = bf16[2,3,128,128]{3,2,1,0:T(8,128)(2,1)S(1)} fusion(bf16[2,3,128,128]{3,2,1,0:T(8,128)(2,1)S(1)} %broadcast_multiply_fusion, s32[1024]{0:T(1024)S(1)} %pad_clamp_fusion.3), kind=kCustom, calls=%fused_computation.1 | custom fusion | bytes 393224 | tf_op jit(solution)/shard_map/gather | solution.py:67
  16.8 0.2 reshape.189
  17.0 0.2 copy.55
  17.2 0.6 %gather_fusion.5 = bf16[6,2,128,128]{3,2,1,0:T(8,128)(2,1)S(1)} fusion(bf16[2,2,128,128]{3,2,1,0:T(8,128)(2,1)S(1)} %bitcast.77, s32[1024]{0:T(1024)S(1)} %pad_clamp_fusion), kind=kCustom, calls=%fused_computation.5 | custom fusion | bytes 786456 | tf_op jit(solution)/shard_map/gather | solution.py:65
  17.8 0.2 fusion.3
  18.1 4.9 %collective-permute-start = (bf16[2,64,128]{2,1,0:T(8,128)(2,1)S(1)}, bf16[2,64,128]{2,1,0:T(8,128)(2,1)S(1)}, u32[]{:S(2)}, u32[]{:S(2)}) collective-permute-start(bf16[2,64,128]{2,1,0:T(8,128)(2,1)S(1)} %get-tuple-element.7), channel_id=1, source_target_pairs={{0,4},{4,8},{8,12},{1,5},{5,9},{9,13},{2,6},{6,10},{10,14},{3,7},{... | collective-permute-start | bytes 98312 | tf_op jit(solution)/shard_map/ppermute | solution.py:13
  23.0 1.9 %collective-permute-start.1 = (bf16[2,64,128]{2,1,0:T(8,128)(2,1)S(1)}, bf16[2,64,128]{2,1,0:T(8,128)(2,1)S(1)}, u32[]{:S(2)}, u32[]{:S(2)}) collective-permute-start(bf16[2,64,128]{2,1,0:T(8,128)(2,1)S(1)} %get-tuple-element.8), channel_id=1, source_target_pairs={{4,0},{8,4},{12,8},{5,1},{9,5},{13,9},{6,2},{10,6},{14,10},{7,3},{... | collective-permute-start | bytes 98312 | tf_op jit(solution)/shard_map/ppermute | solution.py:13
  25.0 3.3 %collective-permute-done.1 = bf16[2,64,128]{2,1,0:T(8,128)(2,1)S(1)} collective-permute-done((bf16[2,64,128]{2,1,0:T(8,128)(2,1)S(1)}, bf16[2,64,128]{2,1,0:T(8,128)(2,1)S(1)}, u32[]{:S(2)}, u32[]{:S(2)}) %collective-permute-start.1) | collective-permute-done | bytes 32800 | tf_op jit(solution)/shard_map/ppermute | solution.py:13
  28.3 0.7 %maximum_bitcast_fusion = bf16[1,2,256,128]{3,2,1,0:T(8,128)(2,1)} fusion(bf16[2,64,128]{2,1,0:T(8,128)(2,1)S(1)} %get-tuple-element.6, bf16[2,128,128]{2,1,0:T(8,128)(2,1)S(1)} %slice.26, bf16[2,64,128]{2,1,0:T(8,128)(2,1)S(1)} %get-tuple-element.5), kind=kLoop, calls=%fused_computation.16 | loop fusion | flops 393216 | bytes 262144 | tf_op jit(solution)/shard_map/broadcast_in_dim | solution.py:72
  (37 shorter events, 1.0 us)
Async XLA Ops:
  0.0 4.2 %copy-start = (bf16[16,128,128]{2,1,0:T(8,128)(2,1)S(1)}, bf16[16,128,128]{2,1,0:T(8,128)(2,1)}, u32[]{:S(2)}) copy-start(bf16[16,128,128]{2,1,0:T(8,128)(2,1)} %param.10) | copy-start | bytes 1572868
  1.0 0.7 %copy-start.2 = (s32[1,4,3]{1,0,2:T(1,128)S(1)}, s32[1,4,3]{1,0,2:T(1,128)}, u32[]{:S(2)}) copy-start(s32[1,4,3]{1,0,2:T(1,128)} %param.11) | copy-start | bytes 148
  1.9 0.7 %copy-start.3 = (s32[1,4,3]{1,0,2:T(1,128)S(1)}, s32[1,4,3]{1,0,2:T(1,128)}, u32[]{:S(2)}) copy-start(s32[1,4,3]{1,0,2:T(1,128)} %param.12) | copy-start | bytes 148
  2.7 0.7 %copy-start.4 = (s32[1,4,3]{1,0,2:T(1,128)S(1)}, s32[1,4,3]{1,0,2:T(1,128)}, u32[]{:S(2)}) copy-start(s32[1,4,3]{1,0,2:T(1,128)} %param.13) | copy-start | bytes 148
  6.2 10.5 %all-to-all-start = ((bf16[4,2,8192]{2,1,0:T(2,128)(2,1)}), bf16[4,2,8192]{2,1,0:T(2,128)(2,1)S(1)}, u32[]{:S(2)}, u32[]{:S(2)}) async-start(bf16[4,2,8192]{2,1,0:T(2,128)(2,1)} %reshape.188), calls=%async_computation | async-start | bytes 262144 | tf_op jit(solution)/shard_map/all_to_all | solution.py:62
  11.6 0.7 %copy-start.5 = (s32[1,2,3]{2,1,0:T(2,128)S(1)}, s32[1,2,3]{2,1,0:T(2,128)}, u32[]{:S(2)}) copy-start(s32[1,2,3]{2,1,0:T(2,128)} %param.16) | copy-start | bytes 76
  12.4 0.7 %copy-start.6 = (s32[1,2,3]{2,1,0:T(2,128)S(1)}, s32[1,2,3]{2,1,0:T(2,128)}, u32[]{:S(2)}) copy-start(s32[1,2,3]{2,1,0:T(2,128)} %param.17) | copy-start | bytes 76
  13.1 0.7 %copy-start.1 = (s32[1,2,3]{2,1,0:T(2,128)S(1)}, s32[1,2,3]{2,1,0:T(2,128)}, u32[]{:S(2)}) copy-start(s32[1,2,3]{2,1,0:T(2,128)} %param.15) | copy-start | bytes 76
  18.1 6.9 %collective-permute-start = (bf16[2,64,128]{2,1,0:T(8,128)(2,1)S(1)}, bf16[2,64,128]{2,1,0:T(8,128)(2,1)S(1)}, u32[]{:S(2)}, u32[]{:S(2)}) collective-permute-start(bf16[2,64,128]{2,1,0:T(8,128)(2,1)S(1)} %get-tuple-element.7), channel_id=1, source_target_pairs={{0,4},{4,8},{8,12},{1,5},{5,9},{9,13},{2,6},{6,10},{10,14},{3,7},{... | collective-permute-start | bytes 98312 | tf_op jit(solution)/shard_map/ppermute | solution.py:13
  23.0 5.2 %collective-permute-start.1 = (bf16[2,64,128]{2,1,0:T(8,128)(2,1)S(1)}, bf16[2,64,128]{2,1,0:T(8,128)(2,1)S(1)}, u32[]{:S(2)}, u32[]{:S(2)}) collective-permute-start(bf16[2,64,128]{2,1,0:T(8,128)(2,1)S(1)} %get-tuple-element.8), channel_id=1, source_target_pairs={{4,0},{8,4},{12,8},{5,1},{9,5},{13,9},{6,2},{10,6},{14,10},{7,3},{... | collective-permute-start | bytes 98312 | tf_op jit(solution)/shard_map/ppermute | solution.py:13
where the time goes:
time: 29.4 us; the launch traced here: 29 us
  starting transfers between devices  12.2 us (41%)
  local copies, waits for them, and re-layouts  11.8 us (40%)
  waiting for transfers between devices  3.26 us (11%)
  other arithmetic  0.91 us (3%)
  matrix products  0.57 us (2%)
    ppermute x2, starting transfers between devices, passed_along(): return lax.ppermute(block, axis, route)  6.83 us
    all_to_all x1, starting transfers between devices, on_device(): lax.all_to_all(along_samples, 'tile', split_axis=2, concat_axis=1, tiled=...  5.41 us
    unnamed x16, local copies, waits for them, and re-layouts  5.14 us
    ppermute x2, waiting for transfers between devices, passed_along(): return lax.ppermute(block, axis, route)  3.26 us
    gather x1, local copies, waits for them, and re-layouts, on_device(): column_bank[column_pick[0]]  1.62 us
    gather x2, local copies, waits for them, and re-layouts, on_device(): picked = line_tiles[:, band_table[every_id]]  1.18 us
    another operation x2, local copies, waits for them, and re-layouts, on_device(): blocks = image.reshape(channels, lin_dev, column_blocks, BLOCK)  1.02 us
    broadcast_in_dim x1, other arithmetic, on_device(): return gridded[None]  0.67 us
  transfers between devices with their start and end apart: 3, of which 1 were waited for; matrix products, arithmetic and copies ran while one was open for 11% of the time, Pallas kernels for 0%

commit v1 on v0

v1 whole, which is shorter than its diff:
```python
import jax
import jax.numpy as jnp
from jax import lax
from jax.experimental import pallas as pl
from jax.experimental.pallas import tpu as pltpu
from jax.sharding import PartitionSpec as P

BLOCK = 128
EDGE = 64
VMEM = pl.BlockSpec(memory_space=pltpu.VMEM)
SMEM = pl.BlockSpec(memory_space=pltpu.SMEM)
ANY = pl.BlockSpec(memory_space=pl.ANY)
HBM = pl.BlockSpec(memory_space=pltpu.HBM)


def each(count, body):
    if count <= 4:
        for i in range(count):
            body(i)
    else:
        pl.loop(0, count)(body)


def shape(*dims, dtype=jnp.bfloat16):
    return jax.ShapeDtypeStruct(dims, dtype)


def params(*arrays):
    held = sum(a.size * a.dtype.itemsize for a in arrays)
    return dict(
        compiler_params=pltpu.CompilerParams(vmem_limit_bytes=2 * held + (1 << 20)),
        cost_estimate=pl.CostEstimate(flops=10**8, bytes_accessed=held, transcendentals=0),
    )


def rows_kernel(index, pick, mask, image_hbm, bank_hbm, *refs):
    *outs, index_s, pick_s, mask_s, image, bank, sems = refs
    pairs = ((index, index_s), (pick, pick_s), (mask, mask_s), (image_hbm, image), (bank_hbm, bank))
    copies = [pltpu.make_async_copy(a, b, sems.at[k]) for k, (a, b) in enumerate(pairs)]
    for copy in copies:
        copy.start()
    for copy in copies:
        copy.wait()
    channels, lines, _ = image.shape[1:]
    tile = lax.axis_index("tile")

    def write(q, out):
        total = jnp.zeros((channels * lines, BLOCK), jnp.float32)
        for b in range(index.shape[0]):
            start = pl.multiple_of(index_s[b, 0, q] * BLOCK, BLOCK)
            source = image[0, :, :, pl.ds(start, BLOCK)].reshape(channels * lines, BLOCK)
            term = jnp.dot(source, bank[pick_s[b, 0, q]], preferred_element_type=jnp.float32)
            total += term * mask_s[b, 0, q].astype(jnp.float32)
        out[...] = total.astype(jnp.bfloat16).reshape(channels, lines, BLOCK)

    if len(outs) > 1:
        for d, out in enumerate(outs):
            write(jnp.bitwise_xor(tile, d), out)
    else:
        each(outs[0].shape[0], lambda q: write(q, outs[0].at[q]))


def weights_kernel(index, pick, mask, bank, high, low, mine, other):
    blocks = high.shape[0]
    for r in range(blocks):
        for s in range(blocks):
            total = jnp.zeros((BLOCK, BLOCK), jnp.float32)
            for b in range(index.shape[2]):
                used = jnp.where(index[0, r, b] == s, mask[0, r, b], 0).astype(jnp.float32)
                total += bank[pick[0, r, b]].astype(jnp.float32) * used
            rounded = total.astype(jnp.bfloat16)
            columns = slice(s * BLOCK, (s + 1) * BLOCK)
            high[r, :, columns] = rounded
            low[r, :, columns] = (total - rounded.astype(jnp.float32)).astype(jnp.bfloat16)
    coefficients(mine, other)


def coefficients(mine, other):
    zone = lax.axis_index("zone")
    row = lax.broadcasted_iota(jnp.int32, (EDGE, BLOCK), 0).astype(jnp.float32)
    feather = (row + 0.5) / EDGE
    lower = zone < lax.axis_size("zone") - 1
    upper = zone > 0
    mine[0] = jnp.where(upper, feather, 1.0)
    other[0] = jnp.where(upper, 1.0 - feather, 0.0)
    mine[1] = jnp.where(lower, 1.0 - feather, 1.0)
    other[1] = jnp.where(lower, feather, 0.0)


def columns_kernel(high, low, *refs):
    *lines, grid, first, second, held = refs
    tile = lax.axis_index("tile")
    channels, depth, _ = lines[0].shape
    for d, ref in enumerate(lines):
        start = pl.multiple_of(jnp.bitwise_xor(tile, d) * depth, depth)
        for c in range(channels):
            held[pl.ds(start, depth), c * BLOCK : (c + 1) * BLOCK] = ref[c]
    source = held[...]
    for r in range(high.shape[0]):
        total = jnp.dot(high[r], source, preferred_element_type=jnp.float32)
        total += jnp.dot(low[r], source, preferred_element_type=jnp.float32)
        for c in range(channels):
            part = total[:, c * BLOCK : (c + 1) * BLOCK].astype(jnp.bfloat16)
            grid[c, r * BLOCK : (r + 1) * BLOCK] = part
    pick_edges(grid, first, second)


def edge_starts(rows):
    even = lax.axis_index("zone") % 2 == 0
    last = rows - EDGE
    return (
        pl.multiple_of(jnp.where(even, last, 0), EDGE),
        pl.multiple_of(jnp.where(even, 0, last), EDGE),
    )


def pick_edges(grid, first, second):
    one, two = edge_starts(grid.shape[1])
    first[...] = grid[:, pl.ds(one, EDGE)]
    second[...] = grid[:, pl.ds(two, EDGE)]


def general_columns_kernel(index, pick, mask, bank, lines, grid, first, second, mine, other):
    tiles, channels, depth, _ = lines.shape
    span = BLOCK // depth

    def block(r):
        for c in range(channels):
            total = jnp.zeros((BLOCK, BLOCK), jnp.float32)
            for b in range(index.shape[2]):
                source = lines[pl.ds(index[0, r, b] * span, span), c].reshape(BLOCK, BLOCK)
                term = jnp.dot(bank[pick[0, r, b]], source, preferred_element_type=jnp.float32)
                total += term * mask[0, r, b].astype(jnp.float32)
            start = pl.multiple_of(r * BLOCK, BLOCK)
            grid[c, pl.ds(start, BLOCK)] = total.astype(jnp.bfloat16)

    each(index.shape[1], block)
    pick_edges(grid, first, second)
    coefficients(mine, other)


def blend_kernel(mine, other, grid, first, second, out, edges, sems):
    rows = grid.shape[1]
    middle = pltpu.make_async_copy(
        grid.at[:, EDGE : rows - EDGE], out.at[0, :, EDGE : rows - EDGE], sems.at[0]
    )
    middle.start()
    copies = [middle]
    even = lax.axis_index("zone") % 2 == 0
    sides = (jnp.where(even, 1, 0), jnp.where(even, 0, 1))
    for k, (came, side, start) in enumerate(zip((first, second), sides, edge_starts(rows))):
        own = grid[:, pl.ds(start, EDGE)].astype(jnp.float32)
        edges[k] = (mine[side] * own + other[side] * came[...].astype(jnp.float32)).astype(jnp.bfloat16)
        copy = pltpu.make_async_copy(edges.at[k], out.at[0, :, pl.ds(start, EDGE)], sems.at[1 + k])
        copy.start()
        copies.append(copy)
    for copy in copies:
        copy.wait()


def on_device(image, row_bank, row_index, row_pick, row_mask, column_bank, column_index, column_pick, column_mask):
    channels, depth, samples = image.shape[1:]
    blocks = row_index.shape[1]
    line_blocks = column_index.shape[1]
    rows = line_blocks * BLOCK
    tiles = lax.axis_size("tile")
    zones = lax.axis_size("zone")
    small = tiles == 4 and blocks == tiles and line_blocks * BLOCK <= 256
    turned = lambda table: jnp.transpose(table, (2, 0, 1))
    panel = shape(channels, depth, BLOCK)
    sent = [panel] * tiles if small else [shape(blocks, channels, depth, BLOCK)]
    along = pl.pallas_call(
        rows_kernel,
        out_shape=sent,
        in_specs=[HBM] * 5,
        out_specs=[VMEM] * len(sent),
        scratch_shapes=[pltpu.SMEM(turned(row_index).shape, jnp.int32)] * 3
        + [pltpu.VMEM(image.shape, image.dtype), pltpu.VMEM(row_bank.shape, row_bank.dtype)]
        + [pltpu.SemaphoreType.DMA((5,))],
        **params(image, row_bank, *sent),
    )(*(pltpu.with_memory_space_constraint(v, pltpu.HBM) for v in (turned(row_index), turned(row_pick), turned(row_mask), image, row_bank)))
    edge = shape(channels, EDGE, BLOCK)
    grid = shape(channels, rows, BLOCK)
    sides = shape(2, EDGE, BLOCK, dtype=jnp.float32)
    if small:
        dense = shape(line_blocks, BLOCK, rows)
        high, low, mine, other = pl.pallas_call(
            weights_kernel,
            out_shape=(dense, dense, sides, sides),
            in_specs=[SMEM] * 3 + [VMEM],
            out_specs=(VMEM,) * 4,
            **params(column_bank, dense, dense, sides, sides),
        )(column_index, column_pick, column_mask, column_bank)
        lines = [along[0]]
        for d in range(1, tiles):
            lines.append(lax.ppermute(along[d], "tile", [(i, i ^ d) for i in range(tiles)]))
        grid, first, second = pl.pallas_call(
            columns_kernel,
            out_shape=(grid, edge, edge),
            in_specs=[VMEM] * (2 + tiles),
            out_specs=(VMEM,) * 3,
            scratch_shapes=[pltpu.VMEM((rows, channels * BLOCK), jnp.bfloat16)],
            **params(dense, dense, *lines, grid),
        )(high, low, *lines)
    else:
        lines = lax.all_to_all(along[0], "tile", split_axis=0, concat_axis=0, tiled=True)
        grid, first, second, mine, other = pl.pallas_call(
            general_columns_kernel,
            out_shape=(grid, edge, edge, sides, sides),
            in_specs=[SMEM] * 3 + [VMEM] * 2,
            out_specs=(VMEM,) * 5,
            **params(column_bank, lines, grid, edge, edge, sides, sides),
        )(column_index, column_pick, column_mask, column_bank, lines)
    second = lax.ppermute(second, "zone", [(z, ((z + 1) ^ 1) - 1 if 0 < ((z + 1) ^ 1) <= zones else zones - 1 - z) for z in range(zones)])
    first = lax.ppermute(first, "zone", [(z, z ^ 1) for z in range(zones)])
    return pl.pallas_call(
        blend_kernel,
        out_shape=shape(1, channels, rows, BLOCK),
        in_specs=[VMEM] * 5,
        out_specs=ANY,
        scratch_shapes=[pltpu.VMEM((2, channels, EDGE, BLOCK), jnp.bfloat16), pltpu.SemaphoreType.DMA((3,))],
        **params(mine, other, grid, first, second),
    )(mine, other, grid, first, second)


def solution(mesh):
    zoned = P(("groups", "zone"), None, None)
    in_specs = (P(("groups", "zone"), None, "tile", None), P(), zoned, zoned, zoned, P(), zoned, zoned, zoned)
    out_specs = P(("groups", "zone"), None, None, "tile")
    return jax.shard_map(on_device, mesh=mesh, in_specs=in_specs, out_specs=out_specs, check_vma=False)
```

time: 29.4 us -> 17.5 us (0.60)
  local copies, waits for them, and re-layouts: 11.8 us -> 0.01 us
  starting transfers between devices: 12.2 us -> 8.02 us
  Pallas kernels: 0 us -> 3.12 us
  waiting for transfers between devices: 3.26 us -> 6.07 us
  other arithmetic: 0.91 us -> 0 us
  matrix products: 0.57 us -> 0 us
    all_to_all x1 -> x0, starting transfers between devices: 5.41 us -> none  [on_device(): lax.all_to_all(along_samples, 'tile', split_axis=2, concat_axis=1, tiled=...]
    unnamed x16 -> x8, local copies, waits for them, and re-layouts: 5.14 us -> 0.01 us
    gather x6 -> x0, local copies, waits for them, and re-layouts: 4.63 us -> none  [the longest x1 1.62 us: on_device(): column_bank[column_pick[0]]]
    pallas_call x0 -> x4, Pallas kernels: none -> 3.12 us  [the longest x1 1.47 us: on_device(): pl.pallas_call(rows_kernel, out_shape=sent, in_specs=[HBM] * 5, out_specs...]
    ppermute x2 -> x5, waiting for transfers between devices: 3.26 us -> 6.07 us  [the longest x3 3.91 us: on_device(): lax.ppermute(along[d], 'tile', [(i, i ^ d) for i in range(tiles)])]
    ppermute x2 -> x5, starting transfers between devices: 6.83 us -> 8.02 us  [the longest x3 4.49 us: on_device(): lax.ppermute(along[d], 'tile', [(i, i ^ d) for i in range(tiles)])]
    another operation x2 -> x0, local copies, waits for them, and re-layouts: 1.02 us -> none  [on_device(): blocks = image.reshape(channels, lin_dev, column_blocks, BLOCK)]
    broadcast_in_dim x1 -> x0, other arithmetic: 0.67 us -> none  [on_device(): return gridded[None]]
  transfers between devices with their start and end apart: 3 -> 5, of which waited for: 1 -> 3; matrix products, arithmetic and copies ran while one was open for 11% -> 0% of each run, Pallas kernels for 0% -> 4%
where the time goes in v1:
time: 17.5 us; the launch traced here: 17.3 us
  starting transfers between devices  8.02 us (46%)
  waiting for transfers between devices  6.07 us (35%)
  Pallas kernels  3.12 us (18%)
    ppermute x3, starting transfers between devices, on_device(): lax.ppermute(along[d], 'tile', [(i, i ^ d) for i in range(tiles)])  4.49 us
    ppermute x3, waiting for transfers between devices, on_device(): lax.ppermute(along[d], 'tile', [(i, i ^ d) for i in range(tiles)])  3.91 us
    ppermute x1, starting transfers between devices, on_device(): first = lax.ppermute(first, 'zone', [(z, z ^ 1) for z in range(zones)])  2.36 us
    ppermute x1, waiting for transfers between devices, on_device(): lax.ppermute(second, 'zone', [(z, (z + 1 ^ 1) - 1 if 0 < z + 1 ^ 1 <= zon...  2.16 us
    pallas_call x1, Pallas kernels, on_device(): pl.pallas_call(rows_kernel, out_shape=sent, in_specs=[HBM] * 5, out_specs...  1.47 us
    ppermute x1, starting transfers between devices, on_device(): lax.ppermute(second, 'zone', [(z, (z + 1 ^ 1) - 1 if 0 < z + 1 ^ 1 <= zon...  1.18 us
    pallas_call x1, Pallas kernels, on_device(): pl.pallas_call(weights_kernel, out_shape=(dense, dense, sides, sides), in...  0.71 us
    pallas_call x1, Pallas kernels, on_device(): pl.pallas_call(blend_kernel, out_shape=shape(1, channels, rows, BLOCK), i...  0.67 us
  transfers between devices with their start and end apart: 5, of which 3 were waited for; matrix products, arithmetic and copies ran while one was open for 0% of the time, Pallas kernels for 4%

profile of v1, /device:TPU:1, one launch (start us, length us, event | category | flops | bytes accessed | tf_op | source)
XLA Modules:
  0.0 17.3 jit_solution(12368384746035037916)
XLA Ops:
  0.0 0.0 copy-start
  0.0 1.5 %shard_map.92 = (bf16[2,64,128]{2,1,0:T(8,128)(2,1)S(1)}, bf16[2,64,128]{2,1,0:T(8,128)(2,1)S(1)}, bf16[2,64,128]{2,1,0:T(8,128)(2,1)S(1)}, bf16[2,64,128]{2,1,0:T(8,128)(2,1)S(1)}) custom-call(s32[3,1,4]{2,1,0:T(1,128)} %bitcast.3, s32[3,1,4]{2,1,0:T(1,128)} %bitcast.4, s32[3,1,4]{2,1,0:T(1,128)} %bitcast.5, bf16[1,2,64,512]{3,2,1,0:T(8,128)(2,1)} %image_hbm.1, ...), custom_call_target="tpu_custom_call" | custom-call | flops 100000000 | bytes 786432 | tf_op jit(solution)/shard_map/pallas_call | solution.py:172
  1.5 2.2 %collective-permute-start = (bf16[2,64,128]{2,1,0:T(8,128)(2,1)S(1)}, bf16[2,64,128]{2,1,0:T(8,128)(2,1)S(1)}, u32[]{:S(2)}, u32[]{:S(2)}) collective-permute-start(bf16[2,64,128]{2,1,0:T(8,128)(2,1)S(1)} %get-tuple-element.21), channel_id=1, source_target_pairs={{0,1},{1,0},{2,3},{3,2},{4,5},{5,4},{6,7},{7,6},{8,9},{9,8},{10,11... | collective-permute-start | bytes 98312 | tf_op jit(solution)/shard_map/ppermute | solution.py:196
  3.7 0.0 copy-start.2
  3.7 0.0 copy-start.3
  3.7 0.0 copy-start.1
  3.7 2.3 %collective-permute-start.1 = (bf16[2,64,128]{2,1,0:T(8,128)(2,1)S(1)}, bf16[2,64,128]{2,1,0:T(8,128)(2,1)S(1)}, u32[]{:S(2)}, u32[]{:S(2)}) collective-permute-start(bf16[2,64,128]{2,1,0:T(8,128)(2,1)S(1)} %get-tuple-element.22), channel_id=1, source_target_pairs={{0,2},{1,3},{2,0},{3,1},{4,6},{5,7},{6,4},{7,5},{8,10},{9,11},{10,... | collective-permute-start | bytes 98312 | tf_op jit(solution)/shard_map/ppermute | solution.py:196
  6.0 0.0 collective-permute-start.2
  6.0 0.0 copy-done
  6.0 0.0 copy-done.2
  6.0 0.0 copy-done.3
  6.0 0.0 copy-done.1
  6.0 0.7 %shard_map.91 = (bf16[2,128,256]{2,1,0:T(8,128)(2,1)S(1)}, bf16[2,128,256]{2,1,0:T(8,128)(2,1)S(1)}, f32[2,64,128]{2,1,0:T(8,128)S(1)}, f32[2,64,128]{2,1,0:T(8,128)S(1)}) custom-call(s32[1,2,3]{2,1,0:T(2,128)S(1)} %copy-done.1, s32[1,2,3]{2,1,0:T(2,128)S(1)} %copy-done.2, s32[1,2,3]{2,1,0:T(2,128)S(1)} %copy-done.3, bf16[16,128,128]{2,1,0:T(8,128)(2,1)S(1)} %copy-done), custom_call_target="tpu_custom_call" | custom-call | flops 100000000 | bytes 917504 | tf_op jit(solution)/shard_map/pallas_call | solution.py:187
  6.7 0.0 collective-permute-done.refs_1_
  6.7 1.0 %collective-permute-done.1.refs_2_ = bf16[2,64,128]{2,1,0:T(8,128)(2,1)S(1)} collective-permute-done((bf16[2,64,128]{2,1,0:T(8,128)(2,1)S(1)}, bf16[2,64,128]{2,1,0:T(8,128)(2,1)S(1)}, u32[]{:S(2)}, u32[]{:S(2)}) %collective-permute-start.1) | collective-permute-done | bytes 32800 | tf_op jit(solution)/shard_map/ppermute | solution.py:196
  7.7 3.0 %collective-permute-done.2.refs_3_ = bf16[2,64,128]{2,1,0:T(8,128)(2,1)S(1)} collective-permute-done((bf16[2,64,128]{2,1,0:T(8,128)(2,1)S(1)}, bf16[2,64,128]{2,1,0:T(8,128)(2,1)S(1)}, u32[]{:S(2)}, u32[]{:S(2)}) %collective-permute-start.2) | collective-permute-done | bytes 32800 | tf_op jit(solution)/shard_map/ppermute | solution.py:196
  10.6 0.3 %shard_map.93 = (bf16[2,256,128]{2,1,0:T(8,128)(2,1)S(1)}, bf16[2,64,128]{2,1,0:T(8,128)(2,1)S(1)}, bf16[2,64,128]{2,1,0:T(8,128)(2,1)S(1)}) custom-call(bf16[2,128,256]{2,1,0:T(8,128)(2,1)S(1)} %get-tuple-element.18.high, bf16[2,128,256]{2,1,0:T(8,128)(2,1)S(1)} %get-tuple-element.19.low, bf16[2,64,128]{2,1,0:T(8,128)(2,1)S(1)} %get-tuple-element.20.refs_0_, ...), custom_call_target="tpu_custom_call" | custom-call | flops 100000000 | bytes 524288 | tf_op jit(solution)/shard_map/pallas_call | solution.py:197
  10.9 2.4 %collective-permute-start.3 = (bf16[2,64,128]{2,1,0:T(8,128)(2,1)S(1)}, bf16[2,64,128]{2,1,0:T(8,128)(2,1)S(1)}, u32[]{:S(2)}, u32[]{:S(2)}) collective-permute-start(bf16[2,64,128]{2,1,0:T(8,128)(2,1)S(1)} %get-tuple-element.25), channel_id=1, source_target_pairs={{0,4},{4,0},{8,12},{12,8},{1,5},{5,1},{9,13},{13,9},{2,6},{6,2},{1... | collective-permute-start | bytes 98312 | tf_op jit(solution)/shard_map/ppermute | solution.py:215
  13.3 1.2 %collective-permute-start.4 = (bf16[2,64,128]{2,1,0:T(8,128)(2,1)S(1)}, bf16[2,64,128]{2,1,0:T(8,128)(2,1)S(1)}, u32[]{:S(2)}, u32[]{:S(2)}) collective-permute-start(bf16[2,64,128]{2,1,0:T(8,128)(2,1)S(1)} %get-tuple-element.26), channel_id=1, source_target_pairs={{0,12},{4,8},{8,4},{12,0},{1,13},{5,9},{9,5},{13,1},{2,14},{6,10},... | collective-permute-start | bytes 98312 | tf_op jit(solution)/shard_map/ppermute | solution.py:214
  14.4 0.0 collective-permute-done.3.first
  14.5 2.2 %collective-permute-done.4.second = bf16[2,64,128]{2,1,0:T(8,128)(2,1)S(1)} collective-permute-done((bf16[2,64,128]{2,1,0:T(8,128)(2,1)S(1)}, bf16[2,64,128]{2,1,0:T(8,128)(2,1)S(1)}, u32[]{:S(2)}, u32[]{:S(2)}) %collective-permute-start.4) | collective-permute-done | bytes 32800 | tf_op jit(solution)/shard_map/ppermute | solution.py:214
  16.6 0.7 %shard_map.94 = bf16[1,2,256,128]{3,2,1,0:T(8,128)(2,1)} custom-call(f32[2,64,128]{2,1,0:T(8,128)S(1)} %get-tuple-element.16.mine, f32[2,64,128]{2,1,0:T(8,128)S(1)} %get-tuple-element.17.other, bf16[2,256,128]{2,1,0:T(8,128)(2,1)S(1)} %get-tuple-element.24.grid, bf16[2,64,128]{2,1,0:T(8,128)(2,1)S(1)} %collective-permute-done.3.first, ...), custom_call_target="tpu_custom_call" | custom-call | flops 100000000 | bytes 327680 | tf_op jit(solution)/shard_map/pallas_call | solution.py:216
Async XLA Ops:
  0.0 6.0 %copy-start = (bf16[16,128,128]{2,1,0:T(8,128)(2,1)S(1)}, bf16[16,128,128]{2,1,0:T(8,128)(2,1)}, u32[]{:S(2)}) copy-start(bf16[16,128,128]{2,1,0:T(8,128)(2,1)} %bank.1) | copy-start | bytes 1572868
  1.5 5.2 %collective-permute-start = (bf16[2,64,128]{2,1,0:T(8,128)(2,1)S(1)}, bf16[2,64,128]{2,1,0:T(8,128)(2,1)S(1)}, u32[]{:S(2)}, u32[]{:S(2)}) collective-permute-start(bf16[2,64,128]{2,1,0:T(8,128)(2,1)S(1)} %get-tuple-element.21), channel_id=1, source_target_pairs={{0,1},{1,0},{2,3},{3,2},{4,5},{5,4},{6,7},{7,6},{8,9},{9,8},{10,11... | collective-permute-start | bytes 98312 | tf_op jit(solution)/shard_map/ppermute | solution.py:196
  3.7 2.3 %copy-start.2 = (s32[1,2,3]{2,1,0:T(2,128)S(1)}, s32[1,2,3]{2,1,0:T(2,128)}, u32[]{:S(2)}) copy-start(s32[1,2,3]{2,1,0:T(2,128)} %pick.1) | copy-start | bytes 76
  3.7 2.3 %copy-start.3 = (s32[1,2,3]{2,1,0:T(2,128)S(1)}, s32[1,2,3]{2,1,0:T(2,128)}, u32[]{:S(2)}) copy-start(s32[1,2,3]{2,1,0:T(2,128)} %mask.1) | copy-start | bytes 76
  3.7 2.3 %copy-start.1 = (s32[1,2,3]{2,1,0:T(2,128)S(1)}, s32[1,2,3]{2,1,0:T(2,128)}, u32[]{:S(2)}) copy-start(s32[1,2,3]{2,1,0:T(2,128)} %index.1) | copy-start | bytes 76
  3.7 4.0 %collective-permute-start.1 = (bf16[2,64,128]{2,1,0:T(8,128)(2,1)S(1)}, bf16[2,64,128]{2,1,0:T(8,128)(2,1)S(1)}, u32[]{:S(2)}, u32[]{:S(2)}) collective-permute-start(bf16[2,64,128]{2,1,0:T(8,128)(2,1)S(1)} %get-tuple-element.22), channel_id=1, source_target_pairs={{0,2},{1,3},{2,0},{3,1},{4,6},{5,7},{6,4},{7,5},{8,10},{9,11},{10,... | collective-permute-start | bytes 98312 | tf_op jit(solution)/shard_map/ppermute | solution.py:196
  6.0 4.7 %collective-permute-start.2 = (bf16[2,64,128]{2,1,0:T(8,128)(2,1)S(1)}, bf16[2,64,128]{2,1,0:T(8,128)(2,1)S(1)}, u32[]{:S(2)}, u32[]{:S(2)}) collective-permute-start(bf16[2,64,128]{2,1,0:T(8,128)(2,1)S(1)} %get-tuple-element.23), channel_id=1, source_target_pairs={{0,3},{1,2},{2,1},{3,0},{4,7},{5,6},{6,5},{7,4},{8,11},{9,10},{10,... | collective-permute-start | bytes 98312 | tf_op jit(solution)/shard_map/ppermute | solution.py:196
  10.9 3.5 %collective-permute-start.3 = (bf16[2,64,128]{2,1,0:T(8,128)(2,1)S(1)}, bf16[2,64,128]{2,1,0:T(8,128)(2,1)S(1)}, u32[]{:S(2)}, u32[]{:S(2)}) collective-permute-start(bf16[2,64,128]{2,1,0:T(8,128)(2,1)S(1)} %get-tuple-element.25), channel_id=1, source_target_pairs={{0,4},{4,0},{8,12},{12,8},{1,5},{5,1},{9,13},{13,9},{2,6},{6,2},{1... | collective-permute-start | bytes 98312 | tf_op jit(solution)/shard_map/ppermute | solution.py:215
  13.3 3.3 %collective-permute-start.4 = (bf16[2,64,128]{2,1,0:T(8,128)(2,1)S(1)}, bf16[2,64,128]{2,1,0:T(8,128)(2,1)S(1)}, u32[]{:S(2)}, u32[]{:S(2)}) collective-permute-start(bf16[2,64,128]{2,1,0:T(8,128)(2,1)S(1)} %get-tuple-element.26), channel_id=1, source_target_pairs={{0,12},{4,8},{8,4},{12,0},{1,13},{5,9},{9,5},{13,1},{2,14},{6,10},... | collective-permute-start | bytes 98312 | tf_op jit(solution)/shard_map/ppermute | solution.py:214

commit v2 on v1

--- a/solution.py
+++ b/solution.py
@@ -5,8 +5,10 @@
 from jax.experimental.pallas import tpu as pltpu
 from jax.sharding import PartitionSpec as P
 
+
 BLOCK = 128
 EDGE = 64
+ROUTES = ((0, 1, 2, 3), (2, 3, 1, 0), (3, 2, 0, 1), (1, 0, 3, 2))
 VMEM = pl.BlockSpec(memory_space=pltpu.VMEM)
 SMEM = pl.BlockSpec(memory_space=pltpu.SMEM)
 ANY = pl.BlockSpec(memory_space=pl.ANY)
@@ -31,6 +33,10 @@
         compiler_params=pltpu.CompilerParams(vmem_limit_bytes=2 * held + (1 << 20)),
         cost_estimate=pl.CostEstimate(flops=10**8, bytes_accessed=held, transcendentals=0),
     )
+
+
+def looked_up(table, place):
+    return sum(jnp.where(place == i, entry, 0) for i, entry in enumerate(table))
 
 
 def rows_kernel(index, pick, mask, image_hbm, bank_hbm, *refs):
@@ -55,7 +61,7 @@
 
     if len(outs) > 1:
         for d, out in enumerate(outs):
-            write(jnp.bitwise_xor(tile, d), out)
+            write(looked_up(ROUTES[d], tile), out)
     else:
         each(outs[0].shape[0], lambda q: write(q, outs[0].at[q]))
 
@@ -92,7 +98,8 @@
     tile = lax.axis_index("tile")
     channels, depth, _ = lines[0].shape
     for d, ref in enumerate(lines):
-        start = pl.multiple_of(jnp.bitwise_xor(tile, d) * depth, depth)
+        came_from = [ROUTES[d].index(i) for i in range(len(lines))]
+        start = pl.multiple_of(looked_up(came_from, tile) * depth, depth)
         for c in range(channels):
             held[pl.ds(start, depth), c * BLOCK : (c + 1) * BLOCK] = ref[c]
     source = held[...]
@@ -121,7 +128,7 @@
 
 
 def general_columns_kernel(index, pick, mask, bank, lines, grid, first, second, mine, other):
-    tiles, channels, depth, _ = lines.shape
+    _, channels, depth, _ = lines.shape
     span = BLOCK // depth
 
     def block(r):
@@ -159,7 +166,7 @@
 
 
 def on_device(image, row_bank, row_index, row_pick, row_mask, column_bank, column_index, column_pick, column_mask):
-    channels, depth, samples = image.shape[1:]
+    channels, depth, _ = image.shape[1:]
     blocks = row_index.shape[1]
     line_blocks = column_index.shape[1]
     rows = line_blocks * BLOCK
@@ -193,7 +200,7 @@
         )(column_index, column_pick, column_mask, column_bank)
         lines = [along[0]]
         for d in range(1, tiles):
-            lines.append(lax.ppermute(along[d], "tile", [(i, i ^ d) for i in range(tiles)]))
+            lines.append(lax.ppermute(along[d], "tile", list(enumerate(ROUTES[d]))))
         grid, first, second = pl.pallas_call(
             columns_kernel,
             out_shape=(grid, edge, edge),

time: 17.5 us -> 15.4 us (0.88)
  waiting for transfers between devices: 6.07 us -> 4.08 us
    ppermute x3, waiting for transfers between devices: 3.91 us -> 1.91 us  [on_device(): lines.append(lax.ppermute(along[d], 'tile', list(enumerate(ROUTES[d]))))]
    ppermute x1, starting transfers between devices: 2.36 us -> 2.18 us  [on_device(): first = lax.ppermute(first, 'zone', [(z, z ^ 1) for z in range(zones)])]
  transfers between devices with their start and end apart: 5 -> 5, of which waited for: 3 -> 4; matrix products, arithmetic and copies ran while one was open for 0% -> 0% of each run, Pallas kernels for 4% -> 5%
where the time goes in v2:
time: 15.4 us; the launch traced here: 15.2 us
  starting transfers between devices  7.9 us (51%)
  waiting for transfers between devices  4.08 us (26%)
  Pallas kernels  3.12 us (20%)
    ppermute x3, starting transfers between devices, on_device(): lines.append(lax.ppermute(along[d], 'tile', list(enumerate(ROUTES[d]))))  4.55 us
    ppermute x1, starting transfers between devices, on_device(): first = lax.ppermute(first, 'zone', [(z, z ^ 1) for z in range(zones)])  2.18 us
    ppermute x1, waiting for transfers between devices, on_device(): lax.ppermute(second, 'zone', [(z, (z + 1 ^ 1) - 1 if 0 < z + 1 ^ 1 <= zon...  2.16 us
    ppermute x3, waiting for transfers between devices, on_device(): lines.append(lax.ppermute(along[d], 'tile', list(enumerate(ROUTES[d]))))  1.91 us
    pallas_call x1, Pallas kernels, on_device(): pl.pallas_call(rows_kernel, out_shape=sent, in_specs=[HBM] * 5, out_specs...  1.47 us
    ppermute x1, starting transfers between devices, on_device(): lax.ppermute(second, 'zone', [(z, (z + 1 ^ 1) - 1 if 0 < z + 1 ^ 1 <= zon...  1.17 us
    pallas_call x1, Pallas kernels, on_device(): pl.pallas_call(weights_kernel, out_shape=(dense, dense, sides, sides), in...  0.71 us
    pallas_call x1, Pallas kernels, on_device(): pl.pallas_call(blend_kernel, out_shape=shape(1, channels, rows, BLOCK), i...  0.67 us
  transfers between devices with their start and end apart: 5, of which 4 were waited for; matrix products, arithmetic and copies ran while one was open for 0% of the time, Pallas kernels for 5%

profile of v2, /device:TPU:1, one launch (start us, length us, event | category | flops | bytes accessed | tf_op | source)
XLA Modules:
  0.0 15.2 jit_solution(10624473790896368617)
XLA Ops:
  0.0 0.0 copy-start
  0.0 1.5 %shard_map.92 = (bf16[2,64,128]{2,1,0:T(8,128)(2,1)S(1)}, bf16[2,64,128]{2,1,0:T(8,128)(2,1)S(1)}, bf16[2,64,128]{2,1,0:T(8,128)(2,1)S(1)}, bf16[2,64,128]{2,1,0:T(8,128)(2,1)S(1)}) custom-call(s32[3,1,4]{2,1,0:T(1,128)} %bitcast.3, s32[3,1,4]{2,1,0:T(1,128)} %bitcast.4, s32[3,1,4]{2,1,0:T(1,128)} %bitcast.5, bf16[1,2,64,512]{3,2,1,0:T(8,128)(2,1)} %image_hbm.1, ...), custom_call_target="tpu_custom_call" | custom-call | flops 100000000 | bytes 786432 | tf_op jit(solution)/shard_map/pallas_call | solution.py:179
  1.5 3.2 %collective-permute-start = (bf16[2,64,128]{2,1,0:T(8,128)(2,1)S(1)}, bf16[2,64,128]{2,1,0:T(8,128)(2,1)S(1)}, u32[]{:S(2)}, u32[]{:S(2)}) collective-permute-start(bf16[2,64,128]{2,1,0:T(8,128)(2,1)S(1)} %get-tuple-element.21), channel_id=1, source_target_pairs={{0,2},{1,3},{2,1},{3,0},{4,6},{5,7},{6,5},{7,4},{8,10},{9,11},{10,... | collective-permute-start | bytes 98312 | tf_op jit(solution)/shard_map/ppermute | solution.py:203
  4.7 0.0 copy-start.2
  4.7 0.0 copy-start.3
  4.7 0.0 copy-start.1
  4.7 1.1 %collective-permute-start.1 = (bf16[2,64,128]{2,1,0:T(8,128)(2,1)S(1)}, bf16[2,64,128]{2,1,0:T(8,128)(2,1)S(1)}, u32[]{:S(2)}, u32[]{:S(2)}) collective-permute-start(bf16[2,64,128]{2,1,0:T(8,128)(2,1)S(1)} %get-tuple-element.22), channel_id=1, source_target_pairs={{0,3},{1,2},{2,0},{3,1},{4,7},{5,6},{6,4},{7,5},{8,11},{9,10},{10,... | collective-permute-start | bytes 98312 | tf_op jit(solution)/shard_map/ppermute | solution.py:203
  5.8 0.3 %collective-permute-start.2 = (bf16[2,64,128]{2,1,0:T(8,128)(2,1)S(1)}, bf16[2,64,128]{2,1,0:T(8,128)(2,1)S(1)}, u32[]{:S(2)}, u32[]{:S(2)}) collective-permute-start(bf16[2,64,128]{2,1,0:T(8,128)(2,1)S(1)} %get-tuple-element.23), channel_id=1, source_target_pairs={{0,1},{1,0},{2,3},{3,2},{4,5},{5,4},{6,7},{7,6},{8,9},{9,8},{10,11... | collective-permute-start | bytes 98312 | tf_op jit(solution)/shard_map/ppermute | solution.py:203
  6.0 0.0 copy-done
  6.0 0.0 copy-done.2
  6.0 0.0 copy-done.3
  6.0 0.0 copy-done.1
  6.1 0.7 %shard_map.91 = (bf16[2,128,256]{2,1,0:T(8,128)(2,1)S(1)}, bf16[2,128,256]{2,1,0:T(8,128)(2,1)S(1)}, f32[2,64,128]{2,1,0:T(8,128)S(1)}, f32[2,64,128]{2,1,0:T(8,128)S(1)}) custom-call(s32[1,2,3]{2,1,0:T(2,128)S(1)} %copy-done.1, s32[1,2,3]{2,1,0:T(2,128)S(1)} %copy-done.2, s32[1,2,3]{2,1,0:T(2,128)S(1)} %copy-done.3, bf16[16,128,128]{2,1,0:T(8,128)(2,1)S(1)} %copy-done), custom_call_target="tpu_custom_call" | custom-call | flops 100000000 | bytes 917504 | tf_op jit(solution)/shard_map/pallas_call | solution.py:194
  6.8 0.2 %collective-permute-done.refs_1_ = bf16[2,64,128]{2,1,0:T(8,128)(2,1)S(1)} collective-permute-done((bf16[2,64,128]{2,1,0:T(8,128)(2,1)S(1)}, bf16[2,64,128]{2,1,0:T(8,128)(2,1)S(1)}, u32[]{:S(2)}, u32[]{:S(2)}) %collective-permute-start) | collective-permute-done | bytes 32800 | tf_op jit(solution)/shard_map/ppermute | solution.py:203
  7.0 1.4 %collective-permute-done.1.refs_2_ = bf16[2,64,128]{2,1,0:T(8,128)(2,1)S(1)} collective-permute-done((bf16[2,64,128]{2,1,0:T(8,128)(2,1)S(1)}, bf16[2,64,128]{2,1,0:T(8,128)(2,1)S(1)}, u32[]{:S(2)}, u32[]{:S(2)}) %collective-permute-start.1) | collective-permute-done | bytes 32800 | tf_op jit(solution)/shard_map/ppermute | solution.py:203
  8.3 0.3 %collective-permute-done.2.refs_3_ = bf16[2,64,128]{2,1,0:T(8,128)(2,1)S(1)} collective-permute-done((bf16[2,64,128]{2,1,0:T(8,128)(2,1)S(1)}, bf16[2,64,128]{2,1,0:T(8,128)(2,1)S(1)}, u32[]{:S(2)}, u32[]{:S(2)}) %collective-permute-start.2) | collective-permute-done | bytes 32800 | tf_op jit(solution)/shard_map/ppermute | solution.py:203
  8.7 0.3 %shard_map.93 = (bf16[2,256,128]{2,1,0:T(8,128)(2,1)S(1)}, bf16[2,64,128]{2,1,0:T(8,128)(2,1)S(1)}, bf16[2,64,128]{2,1,0:T(8,128)(2,1)S(1)}) custom-call(bf16[2,128,256]{2,1,0:T(8,128)(2,1)S(1)} %get-tuple-element.18.high, bf16[2,128,256]{2,1,0:T(8,128)(2,1)S(1)} %get-tuple-element.19.low, bf16[2,64,128]{2,1,0:T(8,128)(2,1)S(1)} %get-tuple-element.20.refs_0_, ...), custom_call_target="tpu_custom_call" | custom-call | flops 100000000 | bytes 524288 | tf_op jit(solution)/shard_map/pallas_call | solution.py:204
  9.0 2.2 %collective-permute-start.3 = (bf16[2,64,128]{2,1,0:T(8,128)(2,1)S(1)}, bf16[2,64,128]{2,1,0:T(8,128)(2,1)S(1)}, u32[]{:S(2)}, u32[]{:S(2)}) collective-permute-start(bf16[2,64,128]{2,1,0:T(8,128)(2,1)S(1)} %get-tuple-element.25), channel_id=1, source_target_pairs={{0,4},{4,0},{8,12},{12,8},{1,5},{5,1},{9,13},{13,9},{2,6},{6,2},{1... | collective-permute-start | bytes 98312 | tf_op jit(solution)/shard_map/ppermute | solution.py:222
  11.1 1.2 %collective-permute-start.4 = (bf16[2,64,128]{2,1,0:T(8,128)(2,1)S(1)}, bf16[2,64,128]{2,1,0:T(8,128)(2,1)S(1)}, u32[]{:S(2)}, u32[]{:S(2)}) collective-permute-start(bf16[2,64,128]{2,1,0:T(8,128)(2,1)S(1)} %get-tuple-element.26), channel_id=1, source_target_pairs={{0,12},{4,8},{8,4},{12,0},{1,13},{5,9},{9,5},{13,1},{2,14},{6,10},... | collective-permute-start | bytes 98312 | tf_op jit(solution)/shard_map/ppermute | solution.py:221
  12.3 0.0 collective-permute-done.3.first
  12.3 2.2 %collective-permute-done.4.second = bf16[2,64,128]{2,1,0:T(8,128)(2,1)S(1)} collective-permute-done((bf16[2,64,128]{2,1,0:T(8,128)(2,1)S(1)}, bf16[2,64,128]{2,1,0:T(8,128)(2,1)S(1)}, u32[]{:S(2)}, u32[]{:S(2)}) %collective-permute-start.4) | collective-permute-done | bytes 32800 | tf_op jit(solution)/shard_map/ppermute | solution.py:221
  14.5 0.7 %shard_map.94 = bf16[1,2,256,128]{3,2,1,0:T(8,128)(2,1)} custom-call(f32[2,64,128]{2,1,0:T(8,128)S(1)} %get-tuple-element.16.mine, f32[2,64,128]{2,1,0:T(8,128)S(1)} %get-tuple-element.17.other, bf16[2,256,128]{2,1,0:T(8,128)(2,1)S(1)} %get-tuple-element.24.grid, bf16[2,64,128]{2,1,0:T(8,128)(2,1)S(1)} %collective-permute-done.3.first, ...), custom_call_target="tpu_custom_call" | custom-call | flops 100000000 | bytes 327680 | tf_op jit(solution)/shard_map/pallas_call | solution.py:223
Async XLA Ops:
  0.0 6.0 %copy-start = (bf16[16,128,128]{2,1,0:T(8,128)(2,1)S(1)}, bf16[16,128,128]{2,1,0:T(8,128)(2,1)}, u32[]{:S(2)}) copy-start(bf16[16,128,128]{2,1,0:T(8,128)(2,1)} %bank.1) | copy-start | bytes 1572868
  1.5 5.5 %collective-permute-start = (bf16[2,64,128]{2,1,0:T(8,128)(2,1)S(1)}, bf16[2,64,128]{2,1,0:T(8,128)(2,1)S(1)}, u32[]{:S(2)}, u32[]{:S(2)}) collective-permute-start(bf16[2,64,128]{2,1,0:T(8,128)(2,1)S(1)} %get-tuple-element.21), channel_id=1, source_target_pairs={{0,2},{1,3},{2,1},{3,0},{4,6},{5,7},{6,5},{7,4},{8,10},{9,11},{10,... | collective-permute-start | bytes 98312 | tf_op jit(solution)/shard_map/ppermute | solution.py:203
  4.7 1.4 %copy-start.2 = (s32[1,2,3]{2,1,0:T(2,128)S(1)}, s32[1,2,3]{2,1,0:T(2,128)}, u32[]{:S(2)}) copy-start(s32[1,2,3]{2,1,0:T(2,128)} %pick.1) | copy-start | bytes 76
  4.7 1.4 %copy-start.3 = (s32[1,2,3]{2,1,0:T(2,128)S(1)}, s32[1,2,3]{2,1,0:T(2,128)}, u32[]{:S(2)}) copy-start(s32[1,2,3]{2,1,0:T(2,128)} %mask.1) | copy-start | bytes 76
  4.7 1.4 %copy-start.1 = (s32[1,2,3]{2,1,0:T(2,128)S(1)}, s32[1,2,3]{2,1,0:T(2,128)}, u32[]{:S(2)}) copy-start(s32[1,2,3]{2,1,0:T(2,128)} %index.1) | copy-start | bytes 76
  4.7 3.7 %collective-permute-start.1 = (bf16[2,64,128]{2,1,0:T(8,128)(2,1)S(1)}, bf16[2,64,128]{2,1,0:T(8,128)(2,1)S(1)}, u32[]{:S(2)}, u32[]{:S(2)}) collective-permute-start(bf16[2,64,128]{2,1,0:T(8,128)(2,1)S(1)} %get-tuple-element.22), channel_id=1, source_target_pairs={{0,3},{1,2},{2,0},{3,1},{4,7},{5,6},{6,4},{7,5},{8,11},{9,10},{10,... | collective-permute-start | bytes 98312 | tf_op jit(solution)/shard_map/ppermute | solution.py:203
  5.8 2.9 %collective-permute-start.2 = (bf16[2,64,128]{2,1,0:T(8,128)(2,1)S(1)}, bf16[2,64,128]{2,1,0:T(8,128)(2,1)S(1)}, u32[]{:S(2)}, u32[]{:S(2)}) collective-permute-start(bf16[2,64,128]{2,1,0:T(8,128)(2,1)S(1)} %get-tuple-element.23), channel_id=1, source_target_pairs={{0,1},{1,0},{2,3},{3,2},{4,5},{5,4},{6,7},{7,6},{8,9},{9,8},{10,11... | collective-permute-start | bytes 98312 | tf_op jit(solution)/shard_map/ppermute | solution.py:203
  9.0 3.4 %collective-permute-start.3 = (bf16[2,64,128]{2,1,0:T(8,128)(2,1)S(1)}, bf16[2,64,128]{2,1,0:T(8,128)(2,1)S(1)}, u32[]{:S(2)}, u32[]{:S(2)}) collective-permute-start(bf16[2,64,128]{2,1,0:T(8,128)(2,1)S(1)} %get-tuple-element.25), channel_id=1, source_target_pairs={{0,4},{4,0},{8,12},{12,8},{1,5},{5,1},{9,13},{13,9},{2,6},{6,2},{1... | collective-permute-start | bytes 98312 | tf_op jit(solution)/shard_map/ppermute | solution.py:222
  11.1 3.3 %collective-permute-start.4 = (bf16[2,64,128]{2,1,0:T(8,128)(2,1)S(1)}, bf16[2,64,128]{2,1,0:T(8,128)(2,1)S(1)}, u32[]{:S(2)}, u32[]{:S(2)}) collective-permute-start(bf16[2,64,128]{2,1,0:T(8,128)(2,1)S(1)} %get-tuple-element.26), channel_id=1, source_target_pairs={{0,12},{4,8},{8,4},{12,0},{1,13},{5,9},{9,5},{13,1},{2,14},{6,10},... | collective-permute-start | bytes 98312 | tf_op jit(solution)/shard_map/ppermute | solution.py:221

commit v3 on v2

--- a/solution.py
+++ b/solution.py
@@ -8,6 +8,7 @@
 
 BLOCK = 128
 EDGE = 64
+SPLIT = 1
 ROUTES = ((0, 1, 2, 3), (2, 3, 1, 0), (3, 2, 0, 1), (1, 0, 3, 2))
 VMEM = pl.BlockSpec(memory_space=pltpu.VMEM)
 SMEM = pl.BlockSpec(memory_space=pltpu.SMEM)
@@ -41,7 +42,11 @@
 
 def rows_kernel(index, pick, mask, image_hbm, bank_hbm, *refs):
     *outs, index_s, pick_s, mask_s, image, bank, sems = refs
-    pairs = ((index, index_s), (pick, pick_s), (mask, mask_s), (image_hbm, image), (bank_hbm, bank))
+    pairs = [(index, index_s), (pick, pick_s), (mask, mask_s)]
+    for k in range(SPLIT):
+        part = pl.ds(k * bank.shape[0] // SPLIT, bank.shape[0] // SPLIT)
+        pairs.append((bank_hbm.at[part], bank.at[part]))
+    pairs.append((image_hbm, image))
     copies = [pltpu.make_async_copy(a, b, sems.at[k]) for k, (a, b) in enumerate(pairs)]
     for copy in copies:
         copy.start()
@@ -51,12 +56,17 @@
     tile = lax.axis_index("tile")
 
     def write(q, out):
-        total = jnp.zeros((channels * lines, BLOCK), jnp.float32)
+        sources, kernels = [], []
         for b in range(index.shape[0]):
             start = pl.multiple_of(index_s[b, 0, q] * BLOCK, BLOCK)
             source = image[0, :, :, pl.ds(start, BLOCK)].reshape(channels * lines, BLOCK)
-            term = jnp.dot(source, bank[pick_s[b, 0, q]], preferred_element_type=jnp.float32)
-            total += term * mask_s[b, 0, q].astype(jnp.float32)
+            sources.append(source * mask_s[b, 0, q].astype(jnp.float32).astype(jnp.bfloat16))
+            kernels.append(bank[pick_s[b, 0, q]])
+        total = jnp.dot(
+            jnp.concatenate(sources, axis=1),
+            jnp.concatenate(kernels, axis=0),
+            preferred_element_type=jnp.float32,
+        )
         out[...] = total.astype(jnp.bfloat16).reshape(channels, lines, BLOCK)
 
     if len(outs) > 1:
@@ -94,7 +104,7 @@
 
 
 def columns_kernel(high, low, *refs):
-    *lines, grid, first, second, held = refs
+    *lines, grid, top, bottom, near, held = refs
     tile = lax.axis_index("tile")
     channels, depth, _ = lines[0].shape
     for d, ref in enumerate(lines):
@@ -109,25 +119,18 @@
         for c in range(channels):
             part = total[:, c * BLOCK : (c + 1) * BLOCK].astype(jnp.bfloat16)
             grid[c, r * BLOCK : (r + 1) * BLOCK] = part
-    pick_edges(grid, first, second)
-
-
-def edge_starts(rows):
-    even = lax.axis_index("zone") % 2 == 0
-    last = rows - EDGE
-    return (
-        pl.multiple_of(jnp.where(even, last, 0), EDGE),
-        pl.multiple_of(jnp.where(even, 0, last), EDGE),
-    )
-
-
-def pick_edges(grid, first, second):
-    one, two = edge_starts(grid.shape[1])
-    first[...] = grid[:, pl.ds(one, EDGE)]
-    second[...] = grid[:, pl.ds(two, EDGE)]
-
-
-def general_columns_kernel(index, pick, mask, bank, lines, grid, first, second, mine, other):
+    pick_edges(grid, top, bottom, near)
+
+
+def pick_edges(grid, top, bottom, near):
+    last = grid.shape[1] - EDGE
+    top[...] = grid[:, :EDGE]
+    bottom[...] = grid[:, last:]
+    start = jnp.where(lax.axis_index("zone") % 2 == 0, last, 0)
+    near[...] = grid[:, pl.ds(pl.multiple_of(start, EDGE), EDGE)]
+
+
+def general_columns_kernel(index, pick, mask, bank, lines, grid, top, bottom, near, mine, other):
     _, channels, depth, _ = lines.shape
     span = BLOCK // depth
 
@@ -142,26 +145,44 @@
             grid[c, pl.ds(start, BLOCK)] = total.astype(jnp.bfloat16)
 
     each(index.shape[1], block)
-    pick_edges(grid, first, second)
+    pick_edges(grid, top, bottom, near)
     coefficients(mine, other)
 
 
-def blend_kernel(mine, other, grid, first, second, out, edges, sems):
+def from_near():
+    zone = lax.axis_index("zone")
+    return (zone % 2 == 1) | (lax.axis_size("zone") % 2 == 1)
+
+
+def blend_kernel(mine, other, grid, below, above, out, edges, sems):
     rows = grid.shape[1]
     middle = pltpu.make_async_copy(
         grid.at[:, EDGE : rows - EDGE], out.at[0, :, EDGE : rows - EDGE], sems.at[0]
     )
     middle.start()
     copies = [middle]
-    even = lax.axis_index("zone") % 2 == 0
-    sides = (jnp.where(even, 1, 0), jnp.where(even, 0, 1))
-    for k, (came, side, start) in enumerate(zip((first, second), sides, edge_starts(rows))):
-        own = grid[:, pl.ds(start, EDGE)].astype(jnp.float32)
-        edges[k] = (mine[side] * own + other[side] * came[...].astype(jnp.float32)).astype(jnp.bfloat16)
-        copy = pltpu.make_async_copy(edges.at[k], out.at[0, :, pl.ds(start, EDGE)], sems.at[1 + k])
+    for k, (came, start) in enumerate(((above, 0), (below, rows - EDGE))):
+        own = grid[:, start : start + EDGE].astype(jnp.float32)
+        mixed = mine[k] * own + other[k] * came[...].astype(jnp.float32)
+        if k == 0:
+            mixed = jnp.where(from_near(), mixed, own)
+        edges[k] = mixed.astype(jnp.bfloat16)
+        copy = pltpu.make_async_copy(edges.at[k], out.at[0, :, start : start + EDGE], sems.at[1 + k])
         copy.start()
         copies.append(copy)
     for copy in copies:
+        copy.wait()
+
+
+def late_kernel(mine, other, grid, above, partial, out, edge, sem):
+    zone = lax.axis_index("zone")
+
+    @pl.when((zone > 0) & ~from_near())
+    def _():
+        own = grid[:, :EDGE].astype(jnp.float32)
+        edge[...] = (mine[0] * own + other[0] * above[...].astype(jnp.float32)).astype(jnp.bfloat16)
+        copy = pltpu.make_async_copy(edge, out.at[0, :, :EDGE], sem)
+        copy.start()
         copy.wait()
 
 
@@ -183,7 +204,7 @@
         out_specs=[VMEM] * len(sent),
         scratch_shapes=[pltpu.SMEM(turned(row_index).shape, jnp.int32)] * 3
         + [pltpu.VMEM(image.shape, image.dtype), pltpu.VMEM(row_bank.shape, row_bank.dtype)]
-        + [pltpu.SemaphoreType.DMA((5,))],
+        + [pltpu.SemaphoreType.DMA((4 + SPLIT,))],
         **params(image, row_bank, *sent),
     )(*(pltpu.with_memory_space_constraint(v, pltpu.HBM) for v in (turned(row_index), turned(row_pick), turned(row_mask), image, row_bank)))
     edge = shape(channels, EDGE, BLOCK)
@@ -201,33 +222,45 @@
         lines = [along[0]]
         for d in range(1, tiles):
             lines.append(lax.ppermute(along[d], "tile", list(enumerate(ROUTES[d]))))
-        grid, first, second = pl.pallas_call(
+        grid, top, bottom, near = pl.pallas_call(
             columns_kernel,
-            out_shape=(grid, edge, edge),
+            out_shape=(grid, edge, edge, edge),
             in_specs=[VMEM] * (2 + tiles),
-            out_specs=(VMEM,) * 3,
+            out_specs=(VMEM,) * 4,
             scratch_shapes=[pltpu.VMEM((rows, channels * BLOCK), jnp.bfloat16)],
             **params(dense, dense, *lines, grid),
         )(high, low, *lines)
     else:
         lines = lax.all_to_all(along[0], "tile", split_axis=0, concat_axis=0, tiled=True)
-        grid, first, second, mine, other = pl.pallas_call(
+        grid, top, bottom, near, mine, other = pl.pallas_call(
             general_columns_kernel,
-            out_shape=(grid, edge, edge, sides, sides),
+            out_shape=(grid, edge, edge, edge, sides, sides),
             in_specs=[SMEM] * 3 + [VMEM] * 2,
-            out_specs=(VMEM,) * 5,
+            out_specs=(VMEM,) * 6,
             **params(column_bank, lines, grid, edge, edge, sides, sides),
         )(column_index, column_pick, column_mask, column_bank, lines)
-    second = lax.ppermute(second, "zone", [(z, ((z + 1) ^ 1) - 1 if 0 < ((z + 1) ^ 1) <= zones else zones - 1 - z) for z in range(zones)])
-    first = lax.ppermute(first, "zone", [(z, z ^ 1) for z in range(zones)])
-    return pl.pallas_call(
+    below = lax.ppermute(top, "zone", [(z, (z - 1) % zones) for z in range(zones)])
+    above = lax.ppermute(bottom, "zone", [(z, (z + 1) % zones) for z in range(zones)])
+    beside = above
+    if zones % 2 == 0:
+        beside = lax.ppermute(near, "zone", [(z, z ^ 1) for z in range(zones)])
+    out = pl.pallas_call(
         blend_kernel,
         out_shape=shape(1, channels, rows, BLOCK),
         in_specs=[VMEM] * 5,
         out_specs=ANY,
         scratch_shapes=[pltpu.VMEM((2, channels, EDGE, BLOCK), jnp.bfloat16), pltpu.SemaphoreType.DMA((3,))],
-        **params(mine, other, grid, first, second),
-    )(mine, other, grid, first, second)
+        **params(mine, other, grid, below, beside),
+    )(mine, other, grid, below, beside)
+    return pl.pallas_call(
+        late_kernel,
+        out_shape=shape(1, channels, rows, BLOCK),
+        in_specs=[VMEM] * 4 + [ANY],
+        out_specs=ANY,
+        input_output_aliases={4: 0},
+        scratch_shapes=[pltpu.VMEM((channels, EDGE, BLOCK), jnp.bfloat16), pltpu.SemaphoreType.DMA],
+        **params(mine, other, grid, above),
+    )(mine, other, grid, above, out)
 
 
 def solution(mesh):

time: 15.4 us -> 15.1 us (0.981)
  the two profiles are of different devices: /device:TPU:1 before, /device:TPU:0 now
where the time goes in v3:
time: 15.1 us; the launch traced here: 14.9 us
  starting transfers between devices  6.39 us (42%)
  waiting for transfers between devices  5.36 us (35%)
  Pallas kernels  3.11 us (21%)
    ppermute x3, starting transfers between devices, on_device(): lines.append(lax.ppermute(along[d], 'tile', list(enumerate(ROUTES[d]))))  5.76 us
    ppermute x3, waiting for transfers between devices, on_device(): lines.append(lax.ppermute(along[d], 'tile', list(enumerate(ROUTES[d]))))  2.79 us
    ppermute x1, waiting for transfers between devices, on_device(): lax.ppermute(bottom, 'zone', [(z, (z + 1) % zones) for z in range(zones)])  1.55 us
    pallas_call x1, Pallas kernels, on_device(): pl.pallas_call(rows_kernel, out_shape=sent, in_specs=[HBM] * 5, out_specs...  1.43 us
    ppermute x1, waiting for transfers between devices, on_device(): lax.ppermute(top, 'zone', [(z, (z - 1) % zones) for z in range(zones)])  1.01 us
    pallas_call x1, Pallas kernels, on_device(): pl.pallas_call(weights_kernel, out_shape=(dense, dense, sides, sides), in...  0.71 us
    pallas_call x1, Pallas kernels, on_device(): pl.pallas_call(blend_kernel, out_shape=shape(1, channels, rows, BLOCK), i...  0.68 us
    ppermute x1, starting transfers between devices, on_device(): beside = lax.ppermute(near, 'zone', [(z, z ^ 1) for z in range(zones)])  0.5 us
  transfers between devices with their start and end apart: 6, of which 5 were waited for; matrix products, arithmetic and copies ran while one was open for 0% of the time, Pallas kernels for 9%

profile of v3, /device:TPU:0, one launch (start us, length us, event | category | flops | bytes accessed | tf_op | source)
XLA Modules:
  0.0 14.9 jit_solution(2516013268490632789)
XLA Ops:
  0.0 0.0 copy-start
  0.0 1.4 %shard_map.92 = (bf16[2,64,128]{2,1,0:T(8,128)(2,1)S(1)}, bf16[2,64,128]{2,1,0:T(8,128)(2,1)S(1)}, bf16[2,64,128]{2,1,0:T(8,128)(2,1)S(1)}, bf16[2,64,128]{2,1,0:T(8,128)(2,1)S(1)}) custom-call(s32[3,1,4]{2,1,0:T(1,128)} %bitcast.3, s32[3,1,4]{2,1,0:T(1,128)} %bitcast.4, s32[3,1,4]{2,1,0:T(1,128)} %bitcast.5, bf16[1,2,64,512]{3,2,1,0:T(8,128)(2,1)} %image_hbm.1, ...), custom_call_target="tpu_custom_call" | custom-call | flops 100000000 | bytes 786432 | tf_op jit(solution)/shard_map/pallas_call | solution.py:200
  1.4 4.1 %collective-permute-start = (bf16[2,64,128]{2,1,0:T(8,128)(2,1)S(1)}, bf16[2,64,128]{2,1,0:T(8,128)(2,1)S(1)}, u32[]{:S(2)}, u32[]{:S(2)}) collective-permute-start(bf16[2,64,128]{2,1,0:T(8,128)(2,1)S(1)} %get-tuple-element.22), channel_id=1, source_target_pairs={{0,2},{1,3},{2,1},{3,0},{4,6},{5,7},{6,5},{7,4},{8,10},{9,11},{10,... | collective-permute-start | bytes 98312 | tf_op jit(solution)/shard_map/ppermute | solution.py:224
  5.6 0.0 copy-start.2
  5.6 0.0 copy-start.3
  5.6 0.0 copy-start.1
  5.6 1.1 %collective-permute-start.1 = (bf16[2,64,128]{2,1,0:T(8,128)(2,1)S(1)}, bf16[2,64,128]{2,1,0:T(8,128)(2,1)S(1)}, u32[]{:S(2)}, u32[]{:S(2)}) collective-permute-start(bf16[2,64,128]{2,1,0:T(8,128)(2,1)S(1)} %get-tuple-element.23), channel_id=1, source_target_pairs={{0,3},{1,2},{2,0},{3,1},{4,7},{5,6},{6,4},{7,5},{8,11},{9,10},{10,... | collective-permute-start | bytes 98312 | tf_op jit(solution)/shard_map/ppermute | solution.py:224
  6.7 0.5 %collective-permute-start.2 = (bf16[2,64,128]{2,1,0:T(8,128)(2,1)S(1)}, bf16[2,64,128]{2,1,0:T(8,128)(2,1)S(1)}, u32[]{:S(2)}, u32[]{:S(2)}) collective-permute-start(bf16[2,64,128]{2,1,0:T(8,128)(2,1)S(1)} %get-tuple-element.24), channel_id=1, source_target_pairs={{0,1},{1,0},{2,3},{3,2},{4,5},{5,4},{6,7},{7,6},{8,9},{9,8},{10,11... | collective-permute-start | bytes 98312 | tf_op jit(solution)/shard_map/ppermute | solution.py:224
  7.2 0.0 copy-done
  7.2 0.0 copy-done.2
  7.2 0.0 copy-done.3
  7.2 0.0 copy-done.1
  7.2 0.7 %shard_map.91 = (bf16[2,128,256]{2,1,0:T(8,128)(2,1)S(1)}, bf16[2,128,256]{2,1,0:T(8,128)(2,1)S(1)}, f32[2,64,128]{2,1,0:T(8,128)S(1)}, f32[2,64,128]{2,1,0:T(8,128)S(1)}) custom-call(s32[1,2,3]{2,1,0:T(2,128)S(1)} %copy-done.1, s32[1,2,3]{2,1,0:T(2,128)S(1)} %copy-done.2, s32[1,2,3]{2,1,0:T(2,128)S(1)} %copy-done.3, bf16[16,128,128]{2,1,0:T(8,128)(2,1)S(1)} %copy-done), custom_call_target="tpu_custom_call" | custom-call | flops 100000000 | bytes 917504 | tf_op jit(solution)/shard_map/pallas_call | solution.py:215
  7.9 0.5 %collective-permute-done.refs_1_ = bf16[2,64,128]{2,1,0:T(8,128)(2,1)S(1)} collective-permute-done((bf16[2,64,128]{2,1,0:T(8,128)(2,1)S(1)}, bf16[2,64,128]{2,1,0:T(8,128)(2,1)S(1)}, u32[]{:S(2)}, u32[]{:S(2)}) %collective-permute-start) | collective-permute-done | bytes 32800 | tf_op jit(solution)/shard_map/ppermute | solution.py:224
  8.5 1.9 %collective-permute-done.1.refs_2_ = bf16[2,64,128]{2,1,0:T(8,128)(2,1)S(1)} collective-permute-done((bf16[2,64,128]{2,1,0:T(8,128)(2,1)S(1)}, bf16[2,64,128]{2,1,0:T(8,128)(2,1)S(1)}, u32[]{:S(2)}, u32[]{:S(2)}) %collective-permute-start.1) | collective-permute-done | bytes 32800 | tf_op jit(solution)/shard_map/ppermute | solution.py:224
  10.4 0.3 %collective-permute-done.2.refs_3_ = bf16[2,64,128]{2,1,0:T(8,128)(2,1)S(1)} collective-permute-done((bf16[2,64,128]{2,1,0:T(8,128)(2,1)S(1)}, bf16[2,64,128]{2,1,0:T(8,128)(2,1)S(1)}, u32[]{:S(2)}, u32[]{:S(2)}) %collective-permute-start.2) | collective-permute-done | bytes 32800 | tf_op jit(solution)/shard_map/ppermute | solution.py:224
  10.7 0.3 %shard_map.93 = (bf16[2,256,128]{2,1,0:T(8,128)(2,1)S(1)}, bf16[2,64,128]{2,1,0:T(8,128)(2,1)S(1)}, bf16[2,64,128]{2,1,0:T(8,128)(2,1)S(1)}, bf16[2,64,128]{2,1,0:T(8,128)(2,1)S(1)}) custom-call(bf16[2,128,256]{2,1,0:T(8,128)(2,1)S(1)} %get-tuple-element.19.high, bf16[2,128,256]{2,1,0:T(8,128)(2,1)S(1)} %get-tuple-element.20.low, ...), custom_call_target="tpu_custom_call" | custom-call | flops 100000000 | bytes 524288 | tf_op jit(solution)/shard_map/pallas_call | solution.py:225
  11.0 0.1 collective-permute-start.4
  11.1 0.5 %collective-permute-start.5 = (bf16[2,64,128]{2,1,0:T(8,128)(2,1)S(1)}, bf16[2,64,128]{2,1,0:T(8,128)(2,1)S(1)}, u32[]{:S(2)}, u32[]{:S(2)}) collective-permute-start(bf16[2,64,128]{2,1,0:T(8,128)(2,1)S(1)} %get-tuple-element.28), channel_id=1, source_target_pairs={{0,4},{4,0},{8,12},{12,8},{1,5},{5,1},{9,13},{13,9},{2,6},{6,2},{1... | collective-permute-start | bytes 98312 | tf_op jit(solution)/shard_map/ppermute | solution.py:246
  11.6 0.1 collective-permute-start.3
  11.7 1.0 %collective-permute-done.4.below = bf16[2,64,128]{2,1,0:T(8,128)(2,1)S(1)} collective-permute-done((bf16[2,64,128]{2,1,0:T(8,128)(2,1)S(1)}, bf16[2,64,128]{2,1,0:T(8,128)(2,1)S(1)}, u32[]{:S(2)}, u32[]{:S(2)}) %collective-permute-start.4) | collective-permute-done | bytes 32800 | tf_op jit(solution)/shard_map/ppermute | solution.py:242
  12.7 0.0 collective-permute-done.5.above
  12.7 0.7 %shard_map.94.partial = bf16[1,2,256,128]{3,2,1,0:T(8,128)(2,1)} custom-call(f32[2,64,128]{2,1,0:T(8,128)S(1)} %get-tuple-element.17.mine, f32[2,64,128]{2,1,0:T(8,128)S(1)} %get-tuple-element.18.other, bf16[2,256,128]{2,1,0:T(8,128)(2,1)S(1)} %get-tuple-element.25.grid, bf16[2,64,128]{2,1,0:T(8,128)(2,1)S(1)} %collective-permute-done.4.below, ...), custom_call_target="tpu_custom_call" | custom-call | flops 100000000 | bytes 327680 | tf_op jit(solution)/shard_map/pallas_call | solution.py:247
  13.4 1.6 %collective-permute-done.3.above = bf16[2,64,128]{2,1,0:T(8,128)(2,1)S(1)} collective-permute-done((bf16[2,64,128]{2,1,0:T(8,128)(2,1)S(1)}, bf16[2,64,128]{2,1,0:T(8,128)(2,1)S(1)}, u32[]{:S(2)}, u32[]{:S(2)}) %collective-permute-start.3) | collective-permute-done | bytes 32800 | tf_op jit(solution)/shard_map/ppermute | solution.py:243
  (1 shorter events, 0.0 us)
Async XLA Ops:
  0.0 7.2 %copy-start = (bf16[16,128,128]{2,1,0:T(8,128)(2,1)S(1)}, bf16[16,128,128]{2,1,0:T(8,128)(2,1)}, u32[]{:S(2)}) copy-start(bf16[16,128,128]{2,1,0:T(8,128)(2,1)} %bank.1) | copy-start | bytes 1572868
  1.4 7.0 %collective-permute-start = (bf16[2,64,128]{2,1,0:T(8,128)(2,1)S(1)}, bf16[2,64,128]{2,1,0:T(8,128)(2,1)S(1)}, u32[]{:S(2)}, u32[]{:S(2)}) collective-permute-start(bf16[2,64,128]{2,1,0:T(8,128)(2,1)S(1)} %get-tuple-element.22), channel_id=1, source_target_pairs={{0,2},{1,3},{2,1},{3,0},{4,6},{5,7},{6,5},{7,4},{8,10},{9,11},{10,... | collective-permute-start | bytes 98312 | tf_op jit(solution)/shard_map/ppermute | solution.py:224
  5.6 1.7 %copy-start.2 = (s32[1,2,3]{2,1,0:T(2,128)S(1)}, s32[1,2,3]{2,1,0:T(2,128)}, u32[]{:S(2)}) copy-start(s32[1,2,3]{2,1,0:T(2,128)} %pick.1) | copy-start | bytes 76
  5.6 1.7 %copy-start.3 = (s32[1,2,3]{2,1,0:T(2,128)S(1)}, s32[1,2,3]{2,1,0:T(2,128)}, u32[]{:S(2)}) copy-start(s32[1,2,3]{2,1,0:T(2,128)} %mask.1) | copy-start | bytes 76
  5.6 1.7 %copy-start.1 = (s32[1,2,3]{2,1,0:T(2,128)S(1)}, s32[1,2,3]{2,1,0:T(2,128)}, u32[]{:S(2)}) copy-start(s32[1,2,3]{2,1,0:T(2,128)} %index.1) | copy-start | bytes 76
  5.6 4.8 %collective-permute-start.1 = (bf16[2,64,128]{2,1,0:T(8,128)(2,1)S(1)}, bf16[2,64,128]{2,1,0:T(8,128)(2,1)S(1)}, u32[]{:S(2)}, u32[]{:S(2)}) collective-permute-start(bf16[2,64,128]{2,1,0:T(8,128)(2,1)S(1)} %get-tuple-element.23), channel_id=1, source_target_pairs={{0,3},{1,2},{2,0},{3,1},{4,7},{5,6},{6,4},{7,5},{8,11},{9,10},{10,... | collective-permute-start | bytes 98312 | tf_op jit(solution)/shard_map/ppermute | solution.py:224
  6.7 4.1 %collective-permute-start.2 = (bf16[2,64,128]{2,1,0:T(8,128)(2,1)S(1)}, bf16[2,64,128]{2,1,0:T(8,128)(2,1)S(1)}, u32[]{:S(2)}, u32[]{:S(2)}) collective-permute-start(bf16[2,64,128]{2,1,0:T(8,128)(2,1)S(1)} %get-tuple-element.24), channel_id=1, source_target_pairs={{0,1},{1,0},{2,3},{3,2},{4,5},{5,4},{6,7},{7,6},{8,9},{9,8},{10,11... | collective-permute-start | bytes 98312 | tf_op jit(solution)/shard_map/ppermute | solution.py:224
  11.0 1.7 %collective-permute-start.4 = (bf16[2,64,128]{2,1,0:T(8,128)(2,1)S(1)}, bf16[2,64,128]{2,1,0:T(8,128)(2,1)S(1)}, u32[]{:S(2)}, u32[]{:S(2)}) collective-permute-start(bf16[2,64,128]{2,1,0:T(8,128)(2,1)S(1)} %get-tuple-element.27), channel_id=1, source_target_pairs={{0,12},{4,0},{8,4},{12,8},{1,13},{5,1},{9,5},{13,9},{2,14},{6,2},{... | collective-permute-start | bytes 98312 | tf_op jit(solution)/shard_map/ppermute | solution.py:242
  11.1 1.6 %collective-permute-start.5 = (bf16[2,64,128]{2,1,0:T(8,128)(2,1)S(1)}, bf16[2,64,128]{2,1,0:T(8,128)(2,1)S(1)}, u32[]{:S(2)}, u32[]{:S(2)}) collective-permute-start(bf16[2,64,128]{2,1,0:T(8,128)(2,1)S(1)} %get-tuple-element.28), channel_id=1, source_target_pairs={{0,4},{4,0},{8,12},{12,8},{1,5},{5,1},{9,13},{13,9},{2,6},{6,2},{1... | collective-permute-start | bytes 98312 | tf_op jit(solution)/shard_map/ppermute | solution.py:246
  11.6 3.3 %collective-permute-start.3 = (bf16[2,64,128]{2,1,0:T(8,128)(2,1)S(1)}, bf16[2,64,128]{2,1,0:T(8,128)(2,1)S(1)}, u32[]{:S(2)}, u32[]{:S(2)}) collective-permute-start(bf16[2,64,128]{2,1,0:T(8,128)(2,1)S(1)} %get-tuple-element.26), channel_id=1, source_target_pairs={{0,4},{4,8},{8,12},{12,0},{1,5},{5,9},{9,13},{13,1},{2,6},{6,10},{... | collective-permute-start | bytes 98312 | tf_op jit(solution)/shard_map/ppermute | solution.py:243
